TPU v7x, 256 devices: a whole 4x4x8 slice. The times are simulated.
256 devices in a mesh: rows: 128 (over x, z, y), cols: 2 (over core).
Axes of the slice: x: 4, y: 4, z: 8, core: 2. Of those that a mesh axis runs over, the one named last changes fastest.
Arguments:
- embeddings: bfloat16 [262144, 384], P('rows')
- test_matrix: bfloat16 [262144, 64], P('rows'), may hold values from -6 to 6
- pair_list: int32 [1024, 2], P(('rows', 'cols')), may hold values from -1 to 255, as said below
Outputs:
- orthonormal_basis: float32 [262144, 64], P(('rows', 'cols'))
- upper_factor: float32 [64, 64], replicated
Inputs may be any that keep to these rules, and one draw needn't show every extreme that they name: `pair_list`: device (r, c) holds 4 entries. Its live entries come first: pairs (i, j) with r * 2 <= i < (r + 1) * 2 and i <= j < min((r + 3) * 2, 256); each pair appears at most once over all devices; its other entries are -1 in both places. The device with c = 0 holds at least one live pair, the two devices of one r hold at most 4 together, and device (0, 0) holds exactly 4.
All inputs are finite; a program needn't handle non-finite values.
Results may differ from a plain program's by a relative error of at most 0.0053.
Values may be sent and summed in bfloat16 or wider, within the bound.
No kernel may reach another device: no remote copies, remote signals or barrier semaphores. Data moves between devices by JAX's collectives and lax.ppermute only.
A program may use at most 64 MiB of HBM per device.

v0:
```python
import jax
import jax.numpy as jnp
from jax import lax
from jax.sharding import PartitionSpec as P

BLK = 1024
SHARPNESS = 6.0
EPSILON = 1e-06


def shifted(value, axis, steps):
    count = lax.axis_size(axis)
    initial, last = (max(0, -steps), min(count, count - steps))
    return lax.ppermute(value, axis, [(source, source + steps) for source in range(initial, last)])


def unit_rows(embeddings):
    widened = embeddings.astype(jnp.float32)
    inverse = lax.rsqrt(jnp.sum(widened * widened, axis=1, keepdims=True) + EPSILON)
    return (widened * inverse).astype(jnp.bfloat16)


def affinity(left_rows, right_rows):
    scores = lax.dot_general(
        left_rows, right_rows, (((1,), (1,)), ((), ())), preferred_element_type=jnp.float32
    )
    return jnp.exp(SHARPNESS * (scores - 1.0)).astype(jnp.bfloat16)


def mirror_product(affinity_tile, vectors):
    return lax.dot_general(
        affinity_tile, vectors, (((0,), (0,)), ((), ())), preferred_element_type=jnp.float32
    )


def block_at(stacked, index):
    return lax.dynamic_index_in_dim(stacked, index, 0, keepdims=False)


def add_block(stacked, index, term):
    return lax.dynamic_update_index_in_dim(stacked, block_at(stacked, index) + term, index, 0)


def count_live(pair_rows):
    return jnp.sum((pair_rows[:, 0] >= 0).astype(jnp.int32))


def orthonormal(sketch_rows, rows_total):
    gram_matrix = lax.dot_general(
        sketch_rows,
        sketch_rows,
        (((0,), (0,)), ((), ())),
        precision=lax.Precision.HIGHEST,
        preferred_element_type=jnp.float32,
    )
    gram_matrix = lax.psum(gram_matrix, ("rows", "cols")) / rows_total
    lower_factor = jnp.linalg.cholesky(gram_matrix)
    solved = lax.linalg.triangular_solve(
        lower_factor, sketch_rows, left_side=False, lower=True, transpose_a=True
    )
    return (solved, lower_factor.T)


def affinity_pass(window_units, own_vectors, my_pairs, base_block):
    blocks_dev = own_vectors.shape[0]
    ahead_vectors = [shifted(own_vectors, "rows", -offset) for offset in (1, 2)]
    window_vectors = jnp.concatenate([own_vectors] + ahead_vectors, axis=0)
    initial = jnp.zeros(window_vectors.shape, jnp.float32)

    def pair_step(slot_index, accumulated):
        entry = my_pairs[slot_index]
        first_block = entry[0] - base_block
        second_block = entry[1] - base_block
        affinity_tile = affinity(
            block_at(window_units, first_block), block_at(window_units, second_block)
        )
        forward = jnp.dot(
            affinity_tile,
            block_at(window_vectors, second_block),
            preferred_element_type=jnp.float32,
        )
        accumulated = add_block(accumulated, first_block, forward)
        mirrored = first_block != second_block

        def add_mirror(current):
            return add_block(
                current,
                second_block,
                mirror_product(affinity_tile, block_at(window_vectors, first_block)),
            )

        return lax.cond(mirrored, add_mirror, lambda unchanged: unchanged, accumulated)

    accumulated = lax.fori_loop(0, count_live(my_pairs), pair_step, initial)
    own_blocks = accumulated[:blocks_dev]
    for offset in (1, 2):
        own_blocks = own_blocks + shifted(
            accumulated[offset * blocks_dev : (offset + 1) * blocks_dev], "rows", offset
        )
    flattened = own_blocks.reshape(-1, own_blocks.shape[2])
    return lax.psum_scatter(flattened, "cols", scatter_dimension=0, tiled=True)


def local(embeddings, test_matrix, pair_list):
    rows_dev = embeddings.shape[0]
    blocks_dev = rows_dev // BLK
    columns = test_matrix.shape[1]
    base_block = lax.axis_index("rows") * blocks_dev
    rows_total = rows_dev * lax.axis_size("rows")
    normed = unit_rows(embeddings).reshape(blocks_dev, BLK, embeddings.shape[1])
    ahead_units = [shifted(normed, "rows", -offset) for offset in (1, 2)]
    window_units = jnp.concatenate([normed] + ahead_units, axis=0)
    sketch_rows = affinity_pass(
        window_units, test_matrix.reshape(blocks_dev, BLK, columns), pair_list, base_block
    )
    panel_rows, _ = orthonormal(sketch_rows, rows_total)
    panel_whole = lax.all_gather(panel_rows.astype(jnp.bfloat16), "cols", axis=0, tiled=True)
    image_rows = affinity_pass(
        window_units, panel_whole.reshape(blocks_dev, BLK, columns), pair_list, base_block
    )
    return orthonormal(image_rows, rows_total)


def solution(mesh):
    in_specs = (P("rows", None), P("rows", None), P(("rows", "cols"), None))
    out_specs = (P(("rows", "cols"), None), P())
    return jax.shard_map(local, mesh=mesh, in_specs=in_specs, out_specs=out_specs, check_vma=False)
```

profile of v0, /device:TPU:1, one launch (start us, length us, event | category | flops | bytes accessed | tf_op | source)
XLA Modules:
  0.0 547.8 jit_solution(13680197383918252103)
XLA Ops:
  7.2 0.0 reduce-scatter.3.cloned.1.call-start
  7.2 1.9 fusion.32
  9.1 0.0 copy-start.1
  9.2 0.0 copy-start.2
  9.2 0.3 fusion.33
  9.5 1.3 collective-permute-start
  10.8 1.3 collective-permute-start.1
  12.1 0.3 copy.14
  12.4 1.3 collective-permute-start.2
  13.7 1.3 collective-permute-start.3
  15.0 0.6 fusion.44
  15.7 85.9 %collective-permute-done.2 = bf16[2,1024,64]{2,1,0:T(8,128)(2,1)S(1)} collective-permute-done((bf16[2,1024,64]{2,1,0:T(8,128)(2,1)S(1)}, bf16[2,1024,64]{2,1,0:T(8,128)(2,1)S(1)}, u32[]{:S(2)}, u32[]{:S(2)}) %collective-permute-start.2) | collective-permute-done | bytes 262176 | tf_op jit(solution)/shard_map/ppermute | solution.py:14
  101.6 0.0 collective-permute-done.3
  101.6 1.5 pad_maximum_fusion.1
  103.1 0.0 collective-permute-done
  103.1 0.0 collective-permute-done.1
  103.1 3.8 pad_maximum_fusion
  106.9 1.3 broadcast.76.clone
  108.3 0.7 while.24
  108.9 1.3 fusion.48
  110.2 6.4 %collective-permute-start.4 = (f32[2,1024,64]{1,2,0:T(8,128)S(1)}, f32[2,1024,64]{1,2,0:T(8,128)S(1)}, u32[]{:S(2)}, u32[]{:S(2)}) collective-permute-start(f32[2,1024,64]{1,2,0:T(8,128)S(1)} %get-tuple-element.272), channel_id=1, source_target_pairs={{0,2},{2,4},{4,6},{6,8},{8,10},{10,12},{12,14},{14,16},{16,18},{18... | collective-permute-start | bytes 1572872 | tf_op jit(solution)/shard_map/ppermute | solution.py:14
  116.6 72.9 %collective-permute-start.5 = (f32[2,1024,64]{1,2,0:T(8,128)S(1)}, f32[2,1024,64]{1,2,0:T(8,128)S(1)}, u32[]{:S(2)}, u32[]{:S(2)}) collective-permute-start(f32[2,1024,64]{1,2,0:T(8,128)S(1)} %get-tuple-element.273), channel_id=1, source_target_pairs={{0,4},{2,6},{4,8},{6,10},{8,12},{10,14},{12,16},{14,18},{16,20},{1... | collective-permute-start | bytes 1572872 | tf_op jit(solution)/shard_map/ppermute | solution.py:14
  189.5 0.0 collective-permute-done.4
  189.5 6.1 %collective-permute-done.5 = f32[2,1024,64]{1,2,0:T(8,128)S(1)} collective-permute-done((f32[2,1024,64]{1,2,0:T(8,128)S(1)}, f32[2,1024,64]{1,2,0:T(8,128)S(1)}, u32[]{:S(2)}, u32[]{:S(2)}) %collective-permute-start.5) | collective-permute-done | bytes 524320 | tf_op jit(solution)/shard_map/ppermute | solution.py:14
  195.6 1.1 add_bitcast_fusion.1
  196.8 0.9 copy.28
  197.6 0.0 reduce-scatter.3.cloned.1.call-update
  197.7 0.0 reduce-scatter.5.cloned.1.call-start
  197.7 36.3 %reduce-scatter.3.cloned.1.call-done = f32[1024,64]{0,1:T(8,128)} async-done(((f32[2048,64]{0,1:T(8,128)}), f32[1024,64]{0,1:T(8,128)}) %reduce-scatter.3.cloned.1.call-update) | async-done | bytes 262160 | tf_op jit(solution)/shard_map/reduce_scatter | solution.py:101
  234.0 1.4 fusion.49
  235.5 77.5 %psum.14 = f32[64,64]{0,1:T(8,128)S(1)} all-reduce(f32[64,64]{0,1:T(8,128)S(1)} %fusion.49), channel_id=1, replica_groups=mesh['rows'=128,'cols'=2] {'rows','cols'}, use_global_device_ids=true, to_apply=%region_7.8 | all-reduce | flops 4096 | bytes 32768 | tf_op jit(solution)/shard_map/psum | solution.py:56
  313.0 0.1 copy.17
  313.1 5.8 %cholesky.44 = f32[64,64]{1,0:T(8,128)S(1)} custom-call(f32[64,64]{1,0:T(8,128)S(1)} %fusion.39), custom_call_target="Cholesky" | custom-call | tf_op jit(solution)/shard_map/jit(cholesky)/cholesky | solution.py:57
  319.0 0.6 compare_reduce_fusion.1
  319.6 0.7 fusion.35
  320.3 4.9 custom-call.6
  325.2 1.4 fusion.34
  326.6 2.5 all_gather.3
  329.1 0.3 copy.27
  329.4 1.3 collective-permute-start.6
  330.7 1.3 collective-permute-start.7
  332.0 22.3 %collective-permute-done.6 = bf16[2,1024,64]{2,1,0:T(8,128)(2,1)S(1)} collective-permute-done((bf16[2,1024,64]{2,1,0:T(8,128)(2,1)S(1)}, bf16[2,1024,64]{2,1,0:T(8,128)(2,1)S(1)}, u32[]{:S(2)}, u32[]{:S(2)}) %collective-permute-start.6) | collective-permute-done | bytes 262176 | tf_op jit(solution)/shard_map/ppermute | solution.py:14
  354.2 0.0 collective-permute-done.7
  354.2 1.5 pad_maximum_fusion.2
  355.8 1.3 broadcast.76
  357.1 0.7 while.25
  357.7 1.3 fusion.47
  359.1 3.7 collective-permute-start.8
  362.7 45.1 %collective-permute-start.9 = (f32[2,1024,64]{1,2,0:T(8,128)S(1)}, f32[2,1024,64]{1,2,0:T(8,128)S(1)}, u32[]{:S(2)}, u32[]{:S(2)}) collective-permute-start(f32[2,1024,64]{1,2,0:T(8,128)S(1)} %get-tuple-element.271), channel_id=1, source_target_pairs={{0,4},{2,6},{4,8},{6,10},{8,12},{10,14},{12,16},{14,18},{16,20},{1... | collective-permute-start | bytes 1572872 | tf_op jit(solution)/shard_map/ppermute | solution.py:14
  407.8 0.0 collective-permute-done.8
  407.8 11.5 %collective-permute-done.9 = f32[2,1024,64]{1,2,0:T(8,128)S(1)} collective-permute-done((f32[2,1024,64]{1,2,0:T(8,128)S(1)}, f32[2,1024,64]{1,2,0:T(8,128)S(1)}, u32[]{:S(2)}, u32[]{:S(2)}) %collective-permute-start.9) | collective-permute-done | bytes 524320 | tf_op jit(solution)/shard_map/ppermute | solution.py:14
  419.3 1.1 add_bitcast_fusion
  420.4 0.8 copy.29
  421.3 0.0 reduce-scatter.5.cloned.1.call-update
  421.3 25.8 %reduce-scatter.5.cloned.1.call-done = f32[1024,64]{0,1:T(8,128)} async-done(((f32[2048,64]{0,1:T(8,128)}), f32[1024,64]{0,1:T(8,128)}) %reduce-scatter.5.cloned.1.call-update) | async-done | bytes 262160 | tf_op jit(solution)/shard_map/reduce_scatter | solution.py:101
  447.1 1.4 fusion.50
  448.4 77.5 %psum.15 = f32[64,64]{0,1:T(8,128)S(1)} all-reduce(f32[64,64]{0,1:T(8,128)S(1)} %fusion.50), channel_id=1, replica_groups=mesh['rows'=128,'cols'=2] {'rows','cols'}, use_global_device_ids=true, to_apply=%region_15.18 | all-reduce | flops 4096 | bytes 32768 | tf_op jit(solution)/shard_map/psum | solution.py:56
  526.0 0.1 copy.23
  526.1 5.8 %cholesky.55 = f32[64,64]{1,0:T(8,128)S(1)} custom-call(f32[64,64]{1,0:T(8,128)S(1)} %fusion.37), custom_call_target="Cholesky" | custom-call | tf_op jit(solution)/shard_map/jit(cholesky)/cholesky | solution.py:57
  532.0 0.6 compare_reduce_fusion
  532.6 0.7 fusion.43
  533.3 4.9 custom-call.7
  538.2 0.7 copy.24
  538.9 2.1 convolution_bitcast_fusion.2
  (11 shorter events, 0.1 us)
Async XLA Ops:
  7.2 2.0 copy-start
  7.2 226.9 %reduce-scatter.3.cloned.1.call-start = ((), (), s32[]{:S(2)}) async-start(), calls=%async_computation.2 | async-start | bytes 786432 | tf_op jit(solution)/shard_map/reduce_scatter | solution.py:101
  9.1 3.0 copy-start.1
  9.2 5.9 %copy-start.2 = (s32[4,2]{0,1:T(2,128)S(1)}, s32[4,2]{0,1:T(2,128)}, u32[]{:S(2)}) copy-start(s32[4,2]{0,1:T(2,128)} %param.16) | copy-start | bytes 100
  9.5 93.6 %collective-permute-start = (bf16[2,1024,384]{2,1,0:T(8,128)(2,1)S(1)}, bf16[2,1024,384]{2,1,0:T(8,128)(2,1)}, u32[]{:S(2)}, u32[]{:S(2)}) collective-permute-start(bf16[2,1024,384]{2,1,0:T(8,128)(2,1)S(1)} %bitcast.145), channel_id=1, source_target_pairs={{2,0},{4,2},{6,4},{8,6},{10,8},{12,10},{14,12},{16,14},{18,16},{20... | collective-permute-start | bytes 4718600 | tf_op jit(solution)/shard_map/ppermute | solution.py:14
  10.8 92.3 %collective-permute-start.1 = (bf16[2,1024,384]{2,1,0:T(8,128)(2,1)S(1)}, bf16[2,1024,384]{2,1,0:T(8,128)(2,1)}, u32[]{:S(2)}, u32[]{:S(2)}) collective-permute-start(bf16[2,1024,384]{2,1,0:T(8,128)(2,1)S(1)} %bitcast.146), channel_id=1, source_target_pairs={{4,0},{6,2},{8,4},{10,6},{12,8},{14,10},{16,12},{18,14},{20,16},{2... | collective-permute-start | bytes 4718600 | tf_op jit(solution)/shard_map/ppermute | solution.py:14
  12.4 89.2 %collective-permute-start.2 = (bf16[2,1024,64]{2,1,0:T(8,128)(2,1)S(1)}, bf16[2,1024,64]{2,1,0:T(8,128)(2,1)S(1)}, u32[]{:S(2)}, u32[]{:S(2)}) collective-permute-start(bf16[2,1024,64]{2,1,0:T(8,128)(2,1)S(1)} %bitcast.150), channel_id=1, source_target_pairs={{2,0},{4,2},{6,4},{8,6},{10,8},{12,10},{14,12},{16,14},{18,16},{20... | collective-permute-start | bytes 786440 | tf_op jit(solution)/shard_map/ppermute | solution.py:14
  13.7 87.9 %collective-permute-start.3 = (bf16[2,1024,64]{2,1,0:T(8,128)(2,1)S(1)}, bf16[2,1024,64]{2,1,0:T(8,128)(2,1)S(1)}, u32[]{:S(2)}, u32[]{:S(2)}) collective-permute-start(bf16[2,1024,64]{2,1,0:T(8,128)(2,1)S(1)} %bitcast.151), channel_id=1, source_target_pairs={{4,0},{6,2},{8,4},{10,6},{12,8},{14,10},{16,12},{18,14},{20,16},{2... | collective-permute-start | bytes 786440 | tf_op jit(solution)/shard_map/ppermute | solution.py:14
  110.2 79.3 %collective-permute-start.4 = (f32[2,1024,64]{1,2,0:T(8,128)S(1)}, f32[2,1024,64]{1,2,0:T(8,128)S(1)}, u32[]{:S(2)}, u32[]{:S(2)}) collective-permute-start(f32[2,1024,64]{1,2,0:T(8,128)S(1)} %get-tuple-element.272), channel_id=1, source_target_pairs={{0,2},{2,4},{4,6},{6,8},{8,10},{10,12},{12,14},{14,16},{16,18},{18... | collective-permute-start | bytes 1572872 | tf_op jit(solution)/shard_map/ppermute | solution.py:14
  116.6 79.0 %collective-permute-start.5 = (f32[2,1024,64]{1,2,0:T(8,128)S(1)}, f32[2,1024,64]{1,2,0:T(8,128)S(1)}, u32[]{:S(2)}, u32[]{:S(2)}) collective-permute-start(f32[2,1024,64]{1,2,0:T(8,128)S(1)} %get-tuple-element.273), channel_id=1, source_target_pairs={{0,4},{2,6},{4,8},{6,10},{8,12},{10,14},{12,16},{14,18},{16,20},{1... | collective-permute-start | bytes 1572872 | tf_op jit(solution)/shard_map/ppermute | solution.py:14
  197.7 249.4 %reduce-scatter.5.cloned.1.call-start = ((), (), s32[]{:S(2)}) async-start(), calls=%async_computation.3 | async-start | bytes 786432 | tf_op jit(solution)/shard_map/reduce_scatter | solution.py:101
  329.4 24.9 %collective-permute-start.6 = (bf16[2,1024,64]{2,1,0:T(8,128)(2,1)S(1)}, bf16[2,1024,64]{2,1,0:T(8,128)(2,1)S(1)}, u32[]{:S(2)}, u32[]{:S(2)}) collective-permute-start(bf16[2,1024,64]{2,1,0:T(8,128)(2,1)S(1)} %bitcast.153), channel_id=1, source_target_pairs={{2,0},{4,2},{6,4},{8,6},{10,8},{12,10},{14,12},{16,14},{18,16},{20... | collective-permute-start | bytes 786440 | tf_op jit(solution)/shard_map/ppermute | solution.py:14
  330.7 23.6 %collective-permute-start.7 = (bf16[2,1024,64]{2,1,0:T(8,128)(2,1)S(1)}, bf16[2,1024,64]{2,1,0:T(8,128)(2,1)S(1)}, u32[]{:S(2)}, u32[]{:S(2)}) collective-permute-start(bf16[2,1024,64]{2,1,0:T(8,128)(2,1)S(1)} %bitcast.154), channel_id=1, source_target_pairs={{4,0},{6,2},{8,4},{10,6},{12,8},{14,10},{16,12},{18,14},{20,16},{2... | collective-permute-start | bytes 786440 | tf_op jit(solution)/shard_map/ppermute | solution.py:14
  359.1 48.8 %collective-permute-start.8 = (f32[2,1024,64]{1,2,0:T(8,128)S(1)}, f32[2,1024,64]{1,2,0:T(8,128)S(1)}, u32[]{:S(2)}, u32[]{:S(2)}) collective-permute-start(f32[2,1024,64]{1,2,0:T(8,128)S(1)} %get-tuple-element.270), channel_id=1, source_target_pairs={{0,2},{2,4},{4,6},{6,8},{8,10},{10,12},{12,14},{14,16},{16,18},{18... | collective-permute-start | bytes 1572872 | tf_op jit(solution)/shard_map/ppermute | solution.py:14
  362.7 56.6 %collective-permute-start.9 = (f32[2,1024,64]{1,2,0:T(8,128)S(1)}, f32[2,1024,64]{1,2,0:T(8,128)S(1)}, u32[]{:S(2)}, u32[]{:S(2)}) collective-permute-start(f32[2,1024,64]{1,2,0:T(8,128)S(1)} %get-tuple-element.271), channel_id=1, source_target_pairs={{0,4},{2,6},{4,8},{6,10},{8,12},{10,14},{12,16},{14,18},{16,20},{1... | collective-permute-start | bytes 1572872 | tf_op jit(solution)/shard_map/ppermute | solution.py:14
Sparse Core Ops, SparseCore 0:
  197.8 36.2 reduce-scatter.2
  421.4 25.5 reduce-scatter.4
where the time goes:
time: 550 us; the launch traced here: 548 us
  waiting for transfers between devices  188 us (34%)
  blocking collectives  158 us (29%)
  starting transfers between devices  136 us (25%)
  other arithmetic  36.2 us (7%)
  between operations  14.3 us (3%)
  local copies, waits for them, and re-layouts  8.38 us (2%)
  matrix products  6.27 us (1%)
    psum x2, blocking collectives, orthonormal(): gram_matrix = lax.psum(gram_matrix, ('rows', 'cols')) / rows_total  155 us
    ppermute x10, starting transfers between devices, shifted(): lax.ppermute(value, axis, [(source, source + steps) for source in range(i...  136 us
    ppermute x10, waiting for transfers between devices, shifted(): lax.ppermute(value, axis, [(source, source + steps) for source in range(i...  126 us
    reduce_scatter x2, waiting for transfers between devices, affinity_pass(): return lax.psum_scatter(flattened, 'cols', scatter_dimension=0, tiled=True)  62.1 us
    another operation x6, other arithmetic, orthonormal(): lower_factor = jnp.linalg.cholesky(gram_matrix)  13 us
  transfers between devices with their start and end apart: 12, of which 6 were waited for; matrix products, arithmetic and copies ran while one was open for 0% of the time, Pallas kernels for 0%

commit v1 on v0

--- a/solution.py
+++ b/solution.py
@@ -6,6 +6,11 @@
 BLK = 1024
 SHARPNESS = 6.0
 EPSILON = 1e-06
+
+
+def advance_the_strings(array_here):
+    now = lax.psum(lax.psum(array_here, axis_name="rows"), "cols")
+    return now
 
 
 def shifted(value, axis, steps):
@@ -53,7 +58,7 @@
         precision=lax.Precision.HIGHEST,
         preferred_element_type=jnp.float32,
     )
-    gram_matrix = lax.psum(gram_matrix, ("rows", "cols")) / rows_total
+    gram_matrix = advance_the_strings(gram_matrix) / rows_total
     lower_factor = jnp.linalg.cholesky(gram_matrix)
     solved = lax.linalg.triangular_solve(
         lower_factor, sketch_rows, left_side=False, lower=True, transpose_a=True

time: 550 us -> 1760 us (3.20)
  blocking collectives: 158 us -> 1390 us
  starting transfers between devices: 136 us -> 117 us
    psum x2 -> x4, blocking collectives: 155 us -> 1380 us  [advance_the_strings(): now = lax.psum(lax.psum(array_here, axis_name='rows'), 'cols')]
    ppermute x10, starting transfers between devices: 136 us -> 117 us  [shifted(): lax.ppermute(value, axis, [(source, source + steps) for source in range(i...]
where the time goes in v1:
time: 1760 us
  blocking collectives  1390 us (79%)
  waiting for transfers between devices  187 us (11%)
  starting transfers between devices  117 us (7%)
  other arithmetic  36.2 us (2%)
    psum x4, blocking collectives, advance_the_strings(): now = lax.psum(lax.psum(array_here, axis_name='rows'), 'cols')  1380 us
    ppermute x10, waiting for transfers between devices, shifted(): lax.ppermute(value, axis, [(source, source + steps) for source in range(i...  121 us
    ppermute x10, starting transfers between devices, shifted(): lax.ppermute(value, axis, [(source, source + steps) for source in range(i...  117 us
    reduce_scatter x2, waiting for transfers between devices, affinity_pass(): return lax.psum_scatter(flattened, 'cols', scatter_dimension=0, tiled=True)  66.1 us
  transfers between devices with their start and end apart: 12, of which 6 were waited for; matrix products, arithmetic and copies ran while one was open for 0% of the time, Pallas kernels for 0%

profile of v1, /device:TPU:1, one launch (start us, length us, event | category | flops | bytes accessed | tf_op | source)
XLA Modules:
  0.0 1757.5 jit_solution(5639679917790080270)
XLA Ops:
  7.2 0.0 reduce-scatter.3.cloned.1.call-start
  7.2 1.9 fusion.32
  9.1 0.0 copy-start.1
  9.2 0.0 copy-start.2
  9.2 0.3 fusion.33
  9.5 1.3 collective-permute-start
  10.8 1.3 collective-permute-start.1
  12.1 0.3 copy.14
  12.4 1.3 collective-permute-start.2
  13.7 1.3 collective-permute-start.3
  15.0 0.6 fusion.44
  15.7 85.9 %collective-permute-done.2 = bf16[2,1024,64]{2,1,0:T(8,128)(2,1)S(1)} collective-permute-done((bf16[2,1024,64]{2,1,0:T(8,128)(2,1)S(1)}, bf16[2,1024,64]{2,1,0:T(8,128)(2,1)S(1)}, u32[]{:S(2)}, u32[]{:S(2)}) %collective-permute-start.2) | collective-permute-done | bytes 262176 | tf_op jit(solution)/shard_map/ppermute | solution.py:19
  101.6 1.5 pad_maximum_fusion.1
  103.1 0.0 collective-permute-done
  103.1 0.0 collective-permute-done.1
  103.1 3.8 pad_maximum_fusion
  106.9 1.3 broadcast.76.clone
  108.3 0.7 while.24
  108.9 1.3 fusion.48
  110.2 6.4 collective-permute-start.4
  116.6 72.6 %collective-permute-start.5 = (f32[2,1024,64]{1,2,0:T(8,128)S(1)}, f32[2,1024,64]{1,2,0:T(8,128)S(1)}, u32[]{:S(2)}, u32[]{:S(2)}) collective-permute-start(f32[2,1024,64]{1,2,0:T(8,128)S(1)} %get-tuple-element.273), channel_id=1, source_target_pairs={{0,4},{2,6},{4,8},{6,10},{8,12},{10,14},{12,16},{14,18},{16,20},{1... | collective-permute-start | bytes 1572872 | tf_op jit(solution)/shard_map/ppermute | solution.py:19
  189.2 0.0 collective-permute-done.4
  189.2 6.1 collective-permute-done.5
  195.4 1.1 add_bitcast_fusion.1
  196.5 0.9 copy.28
  197.4 0.0 reduce-scatter.3.cloned.1.call-update
  197.4 0.0 reduce-scatter.5.cloned.1.call-start
  197.4 36.3 %reduce-scatter.3.cloned.1.call-done = f32[1024,64]{0,1:T(8,128)} async-done(((f32[2048,64]{0,1:T(8,128)}), f32[1024,64]{0,1:T(8,128)}) %reduce-scatter.3.cloned.1.call-update) | async-done | bytes 262160 | tf_op jit(solution)/shard_map/reduce_scatter | solution.py:106
  233.7 1.4 fusion.49
  235.1 579.0 %psum.28 = f32[64,64]{0,1:T(8,128)S(1)} all-reduce(f32[64,64]{0,1:T(8,128)S(1)} %fusion.49), channel_id=1, replica_groups=mesh['rows'=128,'cols'=2] {'rows'}, use_global_device_ids=true, to_apply=%region_7.8 | all-reduce | flops 4096 | bytes 32768 | tf_op jit(solution)/shard_map/psum | solution.py:12
  814.1 113.3 %psum.29 = f32[64,64]{0,1:T(8,128)S(1)} all-reduce(f32[64,64]{0,1:T(8,128)S(1)} %psum.28), channel_id=1, replica_groups=mesh['rows'=128,'cols'=2] {'cols'}, use_global_device_ids=true, to_apply=%region_8.9 | all-reduce | flops 4096 | bytes 32768 | tf_op jit(solution)/shard_map/psum | solution.py:12
  927.4 0.1 copy.17
  927.5 5.8 cholesky.44
  933.4 0.6 compare_reduce_fusion.1
  934.0 0.7 fusion.35
  934.7 4.9 custom-call.6
  939.6 1.4 fusion.34
  941.0 2.0 all_gather.3
  943.0 0.3 copy.27
  943.3 1.3 collective-permute-start.6
  944.6 1.3 collective-permute-start.7
  945.9 22.9 %collective-permute-done.6 = bf16[2,1024,64]{2,1,0:T(8,128)(2,1)S(1)} collective-permute-done((bf16[2,1024,64]{2,1,0:T(8,128)(2,1)S(1)}, bf16[2,1024,64]{2,1,0:T(8,128)(2,1)S(1)}, u32[]{:S(2)}, u32[]{:S(2)}) %collective-permute-start.6) | collective-permute-done | bytes 262176 | tf_op jit(solution)/shard_map/ppermute | solution.py:19
  968.8 0.0 collective-permute-done.7
  968.8 1.5 pad_maximum_fusion.2
  970.3 1.3 broadcast.76
  971.7 0.7 while.25
  972.3 1.3 fusion.47
  973.6 1.3 collective-permute-start.8
  975.0 29.1 %collective-permute-start.9 = (f32[2,1024,64]{1,2,0:T(8,128)S(1)}, f32[2,1024,64]{1,2,0:T(8,128)S(1)}, u32[]{:S(2)}, u32[]{:S(2)}) collective-permute-start(f32[2,1024,64]{1,2,0:T(8,128)S(1)} %get-tuple-element.271), channel_id=1, source_target_pairs={{0,4},{2,6},{4,8},{6,10},{8,12},{10,14},{12,16},{14,18},{16,20},{1... | collective-permute-start | bytes 1572872 | tf_op jit(solution)/shard_map/ppermute | solution.py:19
  1004.0 6.1 collective-permute-done.9
  1010.2 1.1 add_bitcast_fusion
  1011.3 0.8 copy.29
  1012.1 0.0 reduce-scatter.5.cloned.1.call-update
  1012.2 29.8 %reduce-scatter.5.cloned.1.call-done = f32[1024,64]{0,1:T(8,128)} async-done(((f32[2048,64]{0,1:T(8,128)}), f32[1024,64]{0,1:T(8,128)}) %reduce-scatter.5.cloned.1.call-update) | async-done | bytes 262160 | tf_op jit(solution)/shard_map/reduce_scatter | solution.py:106
  1042.0 1.4 fusion.50
  1043.4 579.0 %psum.30 = f32[64,64]{0,1:T(8,128)S(1)} all-reduce(f32[64,64]{0,1:T(8,128)S(1)} %fusion.50), channel_id=1, replica_groups=mesh['rows'=128,'cols'=2] {'rows'}, use_global_device_ids=true, to_apply=%region_16.19 | all-reduce | flops 4096 | bytes 32768 | tf_op jit(solution)/shard_map/psum | solution.py:12
  1622.4 113.3 %psum.31 = f32[64,64]{0,1:T(8,128)S(1)} all-reduce(f32[64,64]{0,1:T(8,128)S(1)} %psum.30), channel_id=1, replica_groups=mesh['rows'=128,'cols'=2] {'cols'}, use_global_device_ids=true, to_apply=%region_17.20 | all-reduce | flops 4096 | bytes 32768 | tf_op jit(solution)/shard_map/psum | solution.py:12
  1735.7 0.1 copy.23
  1735.8 5.8 cholesky.55
  1741.7 0.6 compare_reduce_fusion
  1742.3 0.7 fusion.43
  1743.0 4.9 custom-call.7
  1747.9 0.7 copy.24
  1748.6 2.1 convolution_bitcast_fusion.2
  (13 shorter events, 0.1 us)
Async XLA Ops:
  7.2 2.0 copy-start
  7.2 226.5 %reduce-scatter.3.cloned.1.call-start = ((), (), s32[]{:S(2)}) async-start(), calls=%async_computation.2 | async-start | bytes 786432 | tf_op jit(solution)/shard_map/reduce_scatter | solution.py:106
  9.1 3.0 copy-start.1
  9.2 5.9 copy-start.2
  9.5 93.6 %collective-permute-start = (bf16[2,1024,384]{2,1,0:T(8,128)(2,1)S(1)}, bf16[2,1024,384]{2,1,0:T(8,128)(2,1)}, u32[]{:S(2)}, u32[]{:S(2)}) collective-permute-start(bf16[2,1024,384]{2,1,0:T(8,128)(2,1)S(1)} %bitcast.145), channel_id=1, source_target_pairs={{2,0},{4,2},{6,4},{8,6},{10,8},{12,10},{14,12},{16,14},{18,16},{20... | collective-permute-start | bytes 4718600 | tf_op jit(solution)/shard_map/ppermute | solution.py:19
  10.8 92.3 %collective-permute-start.1 = (bf16[2,1024,384]{2,1,0:T(8,128)(2,1)S(1)}, bf16[2,1024,384]{2,1,0:T(8,128)(2,1)}, u32[]{:S(2)}, u32[]{:S(2)}) collective-permute-start(bf16[2,1024,384]{2,1,0:T(8,128)(2,1)S(1)} %bitcast.146), channel_id=1, source_target_pairs={{4,0},{6,2},{8,4},{10,6},{12,8},{14,10},{16,12},{18,14},{20,16},{2... | collective-permute-start | bytes 4718600 | tf_op jit(solution)/shard_map/ppermute | solution.py:19
  12.4 89.2 %collective-permute-start.2 = (bf16[2,1024,64]{2,1,0:T(8,128)(2,1)S(1)}, bf16[2,1024,64]{2,1,0:T(8,128)(2,1)S(1)}, u32[]{:S(2)}, u32[]{:S(2)}) collective-permute-start(bf16[2,1024,64]{2,1,0:T(8,128)(2,1)S(1)} %bitcast.150), channel_id=1, source_target_pairs={{2,0},{4,2},{6,4},{8,6},{10,8},{12,10},{14,12},{16,14},{18,16},{20... | collective-permute-start | bytes 786440 | tf_op jit(solution)/shard_map/ppermute | solution.py:19
  13.7 87.9 %collective-permute-start.3 = (bf16[2,1024,64]{2,1,0:T(8,128)(2,1)S(1)}, bf16[2,1024,64]{2,1,0:T(8,128)(2,1)S(1)}, u32[]{:S(2)}, u32[]{:S(2)}) collective-permute-start(bf16[2,1024,64]{2,1,0:T(8,128)(2,1)S(1)} %bitcast.151), channel_id=1, source_target_pairs={{4,0},{6,2},{8,4},{10,6},{12,8},{14,10},{16,12},{18,14},{20,16},{2... | collective-permute-start | bytes 786440 | tf_op jit(solution)/shard_map/ppermute | solution.py:19
  110.2 79.0 %collective-permute-start.4 = (f32[2,1024,64]{1,2,0:T(8,128)S(1)}, f32[2,1024,64]{1,2,0:T(8,128)S(1)}, u32[]{:S(2)}, u32[]{:S(2)}) collective-permute-start(f32[2,1024,64]{1,2,0:T(8,128)S(1)} %get-tuple-element.272), channel_id=1, source_target_pairs={{0,2},{2,4},{4,6},{6,8},{8,10},{10,12},{12,14},{14,16},{16,18},{18... | collective-permute-start | bytes 1572872 | tf_op jit(solution)/shard_map/ppermute | solution.py:19
  116.6 78.7 %collective-permute-start.5 = (f32[2,1024,64]{1,2,0:T(8,128)S(1)}, f32[2,1024,64]{1,2,0:T(8,128)S(1)}, u32[]{:S(2)}, u32[]{:S(2)}) collective-permute-start(f32[2,1024,64]{1,2,0:T(8,128)S(1)} %get-tuple-element.273), channel_id=1, source_target_pairs={{0,4},{2,6},{4,8},{6,10},{8,12},{10,14},{12,16},{14,18},{16,20},{1... | collective-permute-start | bytes 1572872 | tf_op jit(solution)/shard_map/ppermute | solution.py:19
  197.4 844.6 %reduce-scatter.5.cloned.1.call-start = ((), (), s32[]{:S(2)}) async-start(), calls=%async_computation.3 | async-start | bytes 786432 | tf_op jit(solution)/shard_map/reduce_scatter | solution.py:106
  943.3 25.5 %collective-permute-start.6 = (bf16[2,1024,64]{2,1,0:T(8,128)(2,1)S(1)}, bf16[2,1024,64]{2,1,0:T(8,128)(2,1)S(1)}, u32[]{:S(2)}, u32[]{:S(2)}) collective-permute-start(bf16[2,1024,64]{2,1,0:T(8,128)(2,1)S(1)} %bitcast.153), channel_id=1, source_target_pairs={{2,0},{4,2},{6,4},{8,6},{10,8},{12,10},{14,12},{16,14},{18,16},{20... | collective-permute-start | bytes 786440 | tf_op jit(solution)/shard_map/ppermute | solution.py:19
  944.6 24.2 %collective-permute-start.7 = (bf16[2,1024,64]{2,1,0:T(8,128)(2,1)S(1)}, bf16[2,1024,64]{2,1,0:T(8,128)(2,1)S(1)}, u32[]{:S(2)}, u32[]{:S(2)}) collective-permute-start(bf16[2,1024,64]{2,1,0:T(8,128)(2,1)S(1)} %bitcast.154), channel_id=1, source_target_pairs={{4,0},{6,2},{8,4},{10,6},{12,8},{14,10},{16,12},{18,14},{20,16},{2... | collective-permute-start | bytes 786440 | tf_op jit(solution)/shard_map/ppermute | solution.py:19
  973.6 30.4 %collective-permute-start.8 = (f32[2,1024,64]{1,2,0:T(8,128)S(1)}, f32[2,1024,64]{1,2,0:T(8,128)S(1)}, u32[]{:S(2)}, u32[]{:S(2)}) collective-permute-start(f32[2,1024,64]{1,2,0:T(8,128)S(1)} %get-tuple-element.270), channel_id=1, source_target_pairs={{0,2},{2,4},{4,6},{6,8},{8,10},{10,12},{12,14},{14,16},{16,18},{18... | collective-permute-start | bytes 1572872 | tf_op jit(solution)/shard_map/ppermute | solution.py:19
  975.0 35.2 %collective-permute-start.9 = (f32[2,1024,64]{1,2,0:T(8,128)S(1)}, f32[2,1024,64]{1,2,0:T(8,128)S(1)}, u32[]{:S(2)}, u32[]{:S(2)}) collective-permute-start(f32[2,1024,64]{1,2,0:T(8,128)S(1)} %get-tuple-element.271), channel_id=1, source_target_pairs={{0,4},{2,6},{4,8},{6,10},{8,12},{10,14},{12,16},{14,18},{16,20},{1... | collective-permute-start | bytes 1572872 | tf_op jit(solution)/shard_map/ppermute | solution.py:19
Sparse Core Ops, SparseCore 0:
  197.5 36.1 reduce-scatter.2
  1012.3 29.6 reduce-scatter.4
